TPU v7x, 512 devices: a whole 4x4x16 slice. The times are simulated.
512 devices in a mesh: box: 32 (over y_lo, z), dir: 16 (over y_hi, x, core).
Axes of the slice: x: 4, y: 4 (y_hi: 2, y_lo: 2; y = y_hi * 2 + y_lo), z: 16, core: 2. Of those that a mesh axis runs over, the one named last changes fastest.
Arguments:
- coarse_field: float32 [2048, 2, 4, 2048], P('box', None, None, 'dir'), may hold values from -6 to 6
- trans_table: float32 [316, 2, 2048], P(None, None, 'dir'), may hold values from -1.5 to 1.5
- partner_ids: int32 [2048, 30], P('box'), may hold values from 0 to 2047, as said below
- partner_types: int32 [2048, 30], P('box'), may hold values from 0 to 315
- partner_count: int32 [2048], P('box'), may hold values from 15 to 30
- child_count: int32 [2048], P('box'), may hold values from 1 to 7, as said below
- child_octant: int32 [8192], P('box'), may hold values from 0 to 7
- dir_angles: float32 [2, 2048], replicated, may hold values from -3.140625 to 3.140625
- stencil_ids: int32 [2048, 4], replicated, may hold values from 0 to 511, as said below
- stencil_weights: float32 [2048, 4], replicated, may hold values from -1.8 to 1.8
Outputs:
- fine_field: float32 [8192, 2, 4, 512], P(('box', 'dir'))
Inputs may be any that keep to these rules, and one draw needn't show every extreme that they name: `partner_ids`: coarse box b sits on a grid whose z coordinate takes the two highest bits of b (the higher one as its bit 1) and whose x and y coordinates take the lower bits in turn (x from bit 0, y from bit 1, x from bit 2, and so on); the slots of b name distinct boxes that are children of neighbours of b's parent and not adjacent to b. `child_count`: each aligned block of 64 coarse boxes has exactly 256 children in all. stencil_ids[c, s] lies within 2 of c // 4, counted circularly over 512 directions.
All inputs are finite; a program needn't handle non-finite values.
Results may differ from a plain program's by a relative error of at most 0.0003.
Values sent between devices are 32-bit elements; how exact they have to be, the bound alone decides.
A program may use at most 64 MiB of HBM per device.

v0:
```python
import jax
import jax.numpy as jnp
from jax import lax
from jax.sharding import PartitionSpec as P

wave_scale = 3.0


def interp_matrix(stencil_ids, stencil_weights, targets):
    matrix = jnp.zeros((stencil_ids.shape[0], targets.shape[0]), jnp.float32)
    for point in range(stencil_ids.shape[1]):
        matrix = matrix + jnp.where(
            stencil_ids[:, point, None] == targets[None, :], stencil_weights[:, point, None], 0.0
        )
    return matrix


def shift_children(coarse_rows, parent_local, child_octant, theta_cols, phi_cols):
    sign_x = 1.0 - 2.0 * (child_octant % 2).astype(jnp.float32)
    sign_y = 1.0 - 2.0 * (child_octant // 2 % 2).astype(jnp.float32)
    sign_z = 1.0 - 2.0 * (child_octant // 4).astype(jnp.float32)
    unit_x = jnp.sin(theta_cols) * jnp.cos(phi_cols)
    unit_y = jnp.sin(theta_cols) * jnp.sin(phi_cols)
    unit_z = jnp.cos(theta_cols)
    phase_angle = wave_scale * (
        sign_x[:, None] * unit_x[None, :]
        + sign_y[:, None] * unit_y[None, :]
        + sign_z[:, None] * unit_z[None, :]
    )
    cosine = jnp.cos(phase_angle)[:, None, :]
    sine = jnp.sin(phase_angle)[:, None, :]
    coarse_count = coarse_rows.shape[0]
    select = (parent_local[:, None] == jnp.arange(coarse_count, dtype=jnp.int32)[None, :]).astype(
        jnp.float32
    )
    flat_rows = coarse_rows.reshape(coarse_count, -1)
    gathered = jnp.dot(
        select, flat_rows, precision=lax.Precision.HIGHEST, preferred_element_type=jnp.float32
    )
    gathered = gathered.reshape((parent_local.shape[0],) + coarse_rows.shape[1:])
    real_part = gathered[:, 0] * cosine + gathered[:, 1] * sine
    imag_part = gathered[:, 1] * cosine - gathered[:, 0] * sine
    return jnp.stack([real_part, imag_part], axis=1)


def per_device(
    coarse_field,
    trans_table,
    partner_ids,
    partner_types,
    partner_count,
    child_count,
    child_octant,
    dir_angles,
    stencil_ids,
    stencil_weights,
):
    box_rows = coarse_field.shape[0]
    source_count = coarse_field.shape[2]
    kc_dev = coarse_field.shape[3]
    full_kc = stencil_ids.shape[0]
    fine_count = full_kc // 4
    type_count = trans_table.shape[0]
    dir_index = lax.axis_index("dir")
    sources = lax.all_gather(coarse_field, "box", axis=0, tiled=True)
    live_mask = (
        jnp.arange(partner_ids.shape[1], dtype=jnp.int32)[None, :] < partner_count[:, None]
    ).astype(jnp.float32)
    flat_sources = sources.reshape(sources.shape[0], -1)
    flat_table = trans_table.reshape(type_count, -1)
    type_range = jnp.arange(type_count, dtype=jnp.int32)

    def translate(running, column):
        part_ids, type_ids, weight = column
        source = jnp.take(flat_sources, part_ids, axis=0).reshape(
            (box_rows, 2, source_count, kc_dev)
        )
        type_pick = (type_ids[:, None] == type_range[None, :]).astype(jnp.float32) * weight[:, None]
        tab_row = jnp.dot(
            type_pick,
            flat_table,
            precision=lax.Precision.HIGHEST,
            preferred_element_type=jnp.float32,
        ).reshape((box_rows, 2, kc_dev))
        table_real = tab_row[:, 0, None, :]
        table_imag = tab_row[:, 1, None, :]
        real_part = table_real * source[:, 0] + table_imag * source[:, 1]
        imag_part = table_real * source[:, 1] - table_imag * source[:, 0]
        return (running + jnp.stack([real_part, imag_part], axis=1), None)

    zeros_init = jnp.zeros(coarse_field.shape, jnp.float32)
    translated, _ = lax.scan(translate, zeros_init, (partner_ids.T, partner_types.T, live_mask.T))
    fine_rows = child_octant.shape[0]
    bounds = jnp.cumsum(child_count)
    parent_local = jnp.sum(
        (bounds[None, :] <= jnp.arange(fine_rows, dtype=jnp.int32)[:, None]).astype(jnp.int32),
        axis=1,
    )
    columns = dir_index * kc_dev + jnp.arange(kc_dev, dtype=jnp.int32)
    shifted = shift_children(
        translated,
        parent_local,
        child_octant,
        jnp.take(dir_angles[0], columns),
        jnp.take(dir_angles[1], columns),
    )
    matrix = interp_matrix(stencil_ids, stencil_weights, jnp.arange(fine_count, dtype=jnp.int32))
    return jnp.einsum(
        "rtnc,cf->rtnf",
        lax.all_to_all(shifted, "dir", split_axis=0, concat_axis=3, tiled=True),
        matrix,
        precision=lax.Precision.HIGHEST,
    )


def solution(mesh):
    placed = (
        P("box", None, None, "dir"),
        P(None, None, "dir"),
        P("box", None),
        P("box", None),
        P("box"),
        P("box"),
        P("box"),
        P(),
        P(),
        P(),
    )
    return jax.shard_map(
        per_device,
        mesh=mesh,
        in_specs=placed,
        out_specs=P(("box", "dir"), None, None, None),
        check_vma=False,
    )
```

profile of v0, /device:TPU:1, one launch (start us, length us, event | category | flops | bytes accessed | tf_op | source)
XLA Modules:
  0.0 431.2 jit_solution(15417730732264246359)
XLA Ops:
  14.6 127.0 %all-gather.2.cloned.1.call-done = f32[2048,2,4,128]{3,2,1,0:T(4,128)} async-done(((f32[64,2,4,128]{3,2,1,0:T(4,128)}), f32[2048,2,4,128]{3,2,1,0:T(4,128)}) %all-gather.2.cloned.1.call-update) | async-done | bytes 8388624 | tf_op jit(solution)/shard_map/all_gather | solution.py:65
  141.6 10.3 %reshape.221 = f32[2048,1024]{1,0:T(8,128)} reshape(f32[2048,2,4,128]{3,2,1,0:T(4,128)} %all-gather.2.cloned.1.call-done) | data formatting | bytes 16777216 | tf_op jit(solution)/shard_map/reshape | solution.py:69
  151.9 218.2 %while.11 = (s32[]{:T(128)}, f32[64,2,4,128]{3,2,1,0:T(4,128)S(1)}, s32[30,64]{1,0:T(8,128)}, f32[30,64]{1,0:T(8,128)S(1)}, f32[316,256]{1,0:T(8,128)S(1)}, /*in...) while((s32[]{:T(128)}, f32[64,2,4,128]{3,2,1,0:T(4,128)S(1)}, ...), condition=%wide.region_3.4_spmd.clone, body=%wide.region_2.3_spmd.clone.sunk | while | flops 62628928 | bytes 3607551 | solution.py:92
  154.5 4.2 gather_fusion
  161.7 4.2 gather_fusion
  176.3 4.2 gather_fusion
  190.8 4.2 gather_fusion
  198.1 4.2 gather_fusion
  205.4 4.2 gather_fusion
  212.7 4.2 gather_fusion
  219.9 4.2 gather_fusion
  234.5 4.2 gather_fusion
  241.8 4.2 gather_fusion
  249.1 4.2 gather_fusion
  256.3 4.2 gather_fusion
  263.6 4.2 gather_fusion
  270.9 4.2 gather_fusion
  278.1 4.2 gather_fusion
  285.4 4.2 gather_fusion
  292.7 4.2 gather_fusion
  300.0 4.2 gather_fusion
  307.2 4.2 gather_fusion
  314.5 4.2 gather_fusion
  321.8 4.2 gather_fusion
  336.4 4.2 gather_fusion
  343.6 4.2 gather_fusion
  350.9 4.2 gather_fusion
  358.2 4.2 gather_fusion
  365.5 4.2 gather_fusion
  372.9 28.3 %all-to-all-start = ((f32[256,2,4,128]{3,2,1,0:T(4,128)}), f32[256,2,4,128]{3,2,1,0:T(4,128)S(1)}, u32[]{:S(2)}, u32[]{:S(2)}) async-start(f32[256,2,4,128]{3,2,1,0:T(4,128)} %copy.25), calls=%async_computation | async-start | bytes 2097152 | tf_op jit(solution)/shard_map/all_to_all | solution.py:110
  401.2 17.2 %all-to-all-done = f32[256,2,4,128]{3,2,1,0:T(4,128)S(1)} async-done(((f32[256,2,4,128]{3,2,1,0:T(4,128)}), f32[256,2,4,128]{3,2,1,0:T(4,128)S(1)}, u32[]{:S(2)}, u32[]{:S(2)}) %all-to-all-start) | async-done | bytes 1048608 | tf_op jit(solution)/shard_map/all_to_all | solution.py:110
  419.2 4.3 fusion.11
  (397 shorter events, 119.6 us)
Async XLA Ops:
  6.5 135.1 %all-gather.2.cloned.1.call-start = ((), (), s32[]{:S(2)}) async-start(), calls=%async_computation.1 | async-start | bytes 8650752 | tf_op jit(solution)/shard_map/all_gather | solution.py:65
  371.0 30.1 %copy-start = (s32[2048,4]{0,1:T(4,128)S(1)}, s32[2048,4]{0,1:T(4,128)}, u32[]{:S(2)}) copy-start(s32[2048,4]{0,1:T(4,128)} %param.22) | copy-start | bytes 98308
  371.0 30.2 %copy-start.1 = (f32[2048,4]{0,1:T(4,128)S(1)}, f32[2048,4]{0,1:T(4,128)}, u32[]{:S(2)}) copy-start(f32[2048,4]{0,1:T(4,128)} %param.23) | copy-start | bytes 98308
  372.9 45.5 %all-to-all-start = ((f32[256,2,4,128]{3,2,1,0:T(4,128)}), f32[256,2,4,128]{3,2,1,0:T(4,128)S(1)}, u32[]{:S(2)}, u32[]{:S(2)}) async-start(f32[256,2,4,128]{3,2,1,0:T(4,128)} %copy.25), calls=%async_computation | async-start | bytes 2097152 | tf_op jit(solution)/shard_map/all_to_all | solution.py:110
Sparse Core Ops, SparseCore 0:
  9.4 132.1 all-gather.1
where the time goes:
time: 436 us; the launch traced here: 431 us
  local copies, waits for them, and re-layouts  172 us (39%)
  waiting for transfers between devices  145 us (33%)
  other arithmetic  54.2 us (12%)
  starting transfers between devices  28.3 us (6%)
  matrix products  16.2 us (4%)
  between operations  13.6 us (3%)
    gather x60, local copies, waits for them, and re-layouts, translate(): jnp.take(flat_sources, part_ids, axis=0)  129 us
    all_gather x1, waiting for transfers between devices, per_device(): sources = lax.all_gather(coarse_field, 'box', axis=0, tiled=True)  127 us
    all_to_all x1, starting transfers between devices, per_device(): lax.all_to_all(shifted, 'dir', split_axis=0, concat_axis=3, tiled=True)  28.3 us
    select_n x60, other arithmetic, translate(): jnp.take(flat_sources, part_ids, axis=0)  24.8 us
    eq x30, local copies, waits for them, and re-layouts, translate(): type_ids[:, None] == type_range[None, :]  20.9 us
    and x30, other arithmetic, translate(): jnp.take(flat_sources, part_ids, axis=0)  20.9 us
    all_to_all x1, waiting for transfers between devices, per_device(): lax.all_to_all(shifted, 'dir', split_axis=0, concat_axis=3, tiled=True)  17.2 us
    dot_general x30, matrix products, translate(): jnp.dot(type_pick, flat_table, precision=lax.Precision.HIGHEST, preferred...  11.3 us
  transfers between devices with their start and end apart: 2, of which 2 were waited for; matrix products, arithmetic and copies ran while one was open for 2% of the time, Pallas kernels for 0%

commit v1 on v0

v1 whole, which is shorter than its diff:
```python
import functools

import jax
import jax.numpy as jnp
from jax import lax
from jax.experimental import pallas as pl
from jax.experimental.pallas import tpu as pltpu
from jax.sharding import PartitionSpec as P

MESH = pl.DeviceIdType.MESH
wave_scale = 3.0

RING = 16
HOPS = 8
TILE = 64
QUAD = 16

REACH = (
    ((8, 0), (1, 8), (2, 8), (3, 8)),
    ((8, 1), (3, 8), (8, 7), (5, 8)),
    ((8, 2), (8, 7), (0, 8), (1, 8)),
    ((8, 3), (6, 8), (8, 1), (3, 8)),
    ((8, 3), (1, 8), (8, 6), (3, 8)),
    ((8, 1), (8, 0), (7, 8), (2, 8)),
    ((8, 5), (7, 8), (8, 3), (1, 8)),
    ((8, 3), (8, 2), (8, 1), (0, 8)),
)


def reach_code(way, origin):
    place = origin % 8
    code = jnp.int32(0)
    for which in range(8):
        packed = sum(REACH[which][quad][way] * 16**quad for quad in range(4))
        code = jnp.where(place == which, jnp.int32(packed), code)
    return code


def place_of(z):
    return z % 2 + 2 * (z // 4 % 2), z // 2 % 2


def z_of(dx, dy):
    return dx % 2 + 2 * dy + 4 * (dx // 2)


def lane_iota(rows=8):
    return lax.broadcasted_iota(jnp.int32, (rows, 128), 1)


def roll_lanes(value, shift):
    shift = shift % 128
    return pltpu.roll(value, shift, 1) if shift else value


def build_interp(me_dir, ids_ref, weights_ref, matrix_ref):
    relative = (ids_ref[...] - 32 * me_dir + 2 + 512) % 512
    weights = weights_ref[...]
    row = lax.broadcasted_iota(jnp.int32, (128, 128), 0)
    for sub in range(4):
        wanted = (row - 32 * ((sub + me_dir) % 4) + 2 + 128) % 128
        total = jnp.zeros((128, 128), jnp.float32)
        for point in range(4):
            hit = relative[point : point + 1, :] == wanted
            total = total + jnp.where(hit, weights[point : point + 1, :], 0.0)
        inner = (wanted >= 2) & (wanted < 34)
        columns = slice(128 * sub, 128 * sub + 128)
        matrix_ref[0:128, columns] = jnp.where(inner, total, 0.0)
        matrix_ref[128:256, columns] = jnp.where(inner, 0.0, total)


def pack_rows(shifted_ref, matrix_ref, send_ref, chunk):
    rows = shifted_ref[pl.ds(16 * chunk, 16)].reshape(128, 512)
    product = lax.dot_general(
        rows,
        matrix_ref[...],
        (((1,), (1,)), ((), ())),
        precision=lax.Precision.HIGHEST,
        preferred_element_type=jnp.float32,
    )
    for owner in range(4):
        edges = None
        for line in range(4):
            at = 32 * owner + 8 * line
            send_ref[4 * chunk + owner, line] = product[at : at + 8, 0:128]
            piece = roll_lanes(product[at : at + 8, 128:256], 4 * line)
            edges = piece if edges is None else edges + piece
        send_ref[4 * chunk + owner, 4] = edges


def assemble(got_ref, out_ref):
    lane = lane_iota()
    group = lane // 32
    near = (lane + 2) % 32 < 4
    for sub in range(4):
        moved = (lane - 32 * sub + 128) % 128
        left_from = (moved + 2) // 32 % 4
        right_from = (moved + 96) // 32 % 4
        take_left = moved % 4 >= 2
        for quarter in range(4):
            left = right = None
            for source in range(4):
                left_at = 4 * quarter + source if source else 4 * ((quarter + 1) % 4)
                right_at = 4 * quarter + source if source < 3 else (4 * quarter + 15) % 16
                left_one, right_one = got_ref[left_at, 4], got_ref[right_at, 4]
                left = left_one if left is None else jnp.where(left_from == source, left_one, left)
                right = (
                    right_one if right is None else jnp.where(right_from == source, right_one, right)
                )
            edges = jnp.where(take_left, left, right)
            for line in range(4):
                main = None
                for at in range(4):
                    one = got_ref[4 * quarter + (at - sub) % 4, line]
                    main = one if main is None else jnp.where(group == at, one, main)
                main = roll_lanes(main, -32 * sub)
                extra = roll_lanes(edges, -(32 * sub + 4 * line))
                value = main + jnp.where(near, extra, 0.0)
                columns = slice(128 * quarter, 128 * quarter + 128)
                out_ref[4 * sub + line, 0, :, columns] = value[0:4]
                out_ref[4 * sub + line, 1, :, columns] = value[4:8]


def broadcast_table(raw_ref, table_ref, type_count):
    def step(tile, carry):
        rows = raw_ref[pl.ds(8 * tile, 8), :]
        for which in range(4):
            for part in range(2):
                at = 2 * which + part
                table_ref[4 * tile + which, part] = jnp.broadcast_to(rows[at : at + 1], (8, 128))
        return carry

    lax.fori_loop(0, type_count // 4, step, 0)
    table_ref[type_count] = jnp.zeros((2, 8, 128), jnp.float32)


def stage_indices(own, type_count, ids_ref, types_ref, count_ref, child_ref, octant_ref, stage_ref):
    slots = ids_ref.shape[0]
    slot = lax.broadcasted_iota(jnp.int32, (slots, TILE), 0)
    box = lax.broadcasted_iota(jnp.int32, (slots, TILE), 1)
    live = slot < count_ref[...]
    stage_ref[0:slots, 0:TILE] = jnp.where(live, ids_ref[...], own + box)
    stage_ref[32 : 32 + slots, 0:TILE] = jnp.where(live, types_ref[...], type_count)
    upto = lax.broadcasted_iota(jnp.int32, (TILE, TILE), 0)
    which = lax.broadcasted_iota(jnp.int32, (TILE, TILE), 1)
    bounds = jnp.sum(jnp.where(which <= upto, child_ref[...], 0), axis=1, keepdims=True)
    for half in range(2):
        fine = lax.broadcasted_iota(jnp.int32, (TILE, 128), 1) + 128 * half
        parent = jnp.sum(jnp.where(bounds <= fine, 1, 0), axis=0, keepdims=True)
        stage_ref[64 + half : 65 + half, :] = jnp.minimum(parent, TILE - 1)
    stage_ref[66:68, :] = octant_ref[...]


def build_phases(angle_ref, phase_ref):
    theta, phi = angle_ref[0:1, :], angle_ref[1:2, :]
    unit_x = jnp.sin(theta) * jnp.cos(phi)
    unit_y = jnp.sin(theta) * jnp.sin(phi)
    unit_z = jnp.cos(theta)
    octant = lax.broadcasted_iota(jnp.int32, (8, 128), 0)
    sign_x = 1.0 - 2.0 * (octant % 2).astype(jnp.float32)
    sign_y = 1.0 - 2.0 * (octant // 2 % 2).astype(jnp.float32)
    sign_z = 1.0 - 2.0 * (octant // 4).astype(jnp.float32)
    angle = wave_scale * (sign_x * unit_x + sign_y * unit_y + sign_z * unit_z)
    cosine, sine = jnp.cos(angle), jnp.sin(angle)
    for which in range(8):
        phase_ref[which, 0] = jnp.broadcast_to(cosine[which : which + 1], (8, 128))
        spread = jnp.broadcast_to(sine[which : which + 1], (8, 128))
        phase_ref[which, 1] = jnp.where(octant < 4, spread, -spread)


def translate_boxes(slots, index_ref, field_ref, table_ref, moved_ref):
    real_row = lax.broadcasted_iota(jnp.int32, (8, 128), 0) < 4

    def step(box, carry):
        sums = [None] * 4
        for slot in range(slots):
            source = field_ref[index_ref[slot, box] & (field_ref.shape[0] - 1)]
            kind = index_ref[32 + slot, box] & (table_ref.shape[0] - 1)
            for part in range(2):
                term = table_ref[kind, part] * source
                at = 2 * (slot % 2) + part
                sums[at] = term if sums[at] is None else sums[at] + term
        straight = sums[0] if sums[2] is None else sums[0] + sums[2]
        crossed = sums[1] if sums[3] is None else sums[1] + sums[3]
        crossed = pltpu.roll(crossed, 4, 0)
        value = straight + jnp.where(real_row, crossed, -crossed)
        moved_ref[box, 0] = value
        moved_ref[box, 1] = pltpu.roll(value, 4, 0)
        return carry

    lax.fori_loop(0, TILE, step, 0)


def shift_children(index_ref, moved_ref, phase_ref, shifted_ref):
    def step(owner, carry):
        for fine in range(16):
            sub, line = fine // 4, fine % 4
            at = 16 * owner + fine
            parent = index_ref[64 + at // 128, at % 128] & (TILE - 1)
            octant = index_ref[66 + at // 128, at % 128] & 7
            value = (
                moved_ref[parent, 0] * phase_ref[octant, 0]
                + moved_ref[parent, 1] * phase_ref[octant, 1]
            )
            shifted_ref[4 * owner + line, :, 128 * sub : 128 * sub + 128] = value
        return carry

    lax.fori_loop(0, 16, step, 0)


def kernel(
    type_count,
    x_hbm,
    table_hbm,
    ids_hbm,
    types_hbm,
    count_hbm,
    child_hbm,
    octant_hbm,
    angles_hbm,
    stencil_hbm,
    weights_hbm,
    out_ref,
    field,
    raw,
    table,
    ids,
    types,
    count,
    child,
    octant,
    angles,
    stencil,
    weights,
    stage,
    index,
    phase,
    moved,
    shifted,
    matrix,
    outbox,
    inbox,
    load_sem,
    stage_sem,
    ring_send,
    ring_recv,
    side_send,
    side_recv,
    swap_send,
    swap_recv,
):
    me_box, me_dir = lax.axis_index("box"), lax.axis_index("dir")
    z, plane = me_box % RING, me_box // RING
    dx, dy = place_of(z)
    own = TILE * me_box
    slots = ids_hbm.shape[0]
    up, down = (z + 1) % RING, (z + RING - 1) % RING

    here = pl.ds(pl.multiple_of(128 * me_dir, 128), 128)
    loads = [
        pltpu.make_async_copy(src, dst, load_sem.at[at])
        for at, (src, dst) in enumerate(
            (
                (x_hbm, field.at[pl.ds(own, TILE)]),
                (table_hbm, raw),
                (ids_hbm, ids),
                (types_hbm, types),
                (count_hbm, count),
                (child_hbm, child),
                (octant_hbm, octant),
                (angles_hbm.at[:, here], angles),
                (stencil_hbm.at[:, here], stencil),
                (weights_hbm.at[:, here], weights),
            )
        )
    ]
    for load in loads:
        load.start()

    barrier = pltpu.get_barrier_semaphore()
    for place in (up, down):
        pl.semaphore_signal(
            barrier, inc=1, device_id={"box": RING * plane + place}, device_id_type=MESH
        )
    pl.semaphore_signal(
        barrier, inc=1, device_id={"box": RING * (1 - plane) + z}, device_id_type=MESH
    )
    for step in range(1, 16):
        pl.semaphore_signal(
            barrier, inc=1, device_id={"dir": (me_dir + step) % 16}, device_id_type=MESH
        )
    pl.semaphore_wait(barrier, 18)

    def rows_of(which_plane, origin, start, size):
        return field.at[pl.ds(TILE * (RING * which_plane + origin) + start, size)]

    def hop(way, step, quad, origin, first=False):
        rows = rows_of(plane, origin, QUAD * quad, QUAD)
        return pltpu.make_async_remote_copy(
            src_ref=x_hbm.at[pl.ds(QUAD * quad, QUAD)] if first else rows,
            dst_ref=rows,
            send_sem=ring_send.at[way, step, quad],
            recv_sem=ring_recv.at[way, step, quad],
            device_id={"box": RING * plane + (down if way else up)},
            device_id_type=MESH,
        )

    def side(which_plane, origin, start, size, quad, part, first=False):
        rows = rows_of(which_plane, origin, start, size)
        return pltpu.make_async_remote_copy(
            src_ref=x_hbm.at[pl.ds(start, size)] if first else rows,
            dst_ref=rows,
            send_sem=side_send.at[origin, quad, part],
            recv_sem=side_recv.at[origin, quad, part],
            device_id={"box": RING * (1 - plane) + z},
            device_id_type=MESH,
        )

    for quad in (0, 3, 1, 2):
        for way in range(2):
            far = reach_code(way, z) // 16**quad % 16

            @pl.when(far > 0)
            def _():
                hop(way, 0, quad, z, True).start()

    for quad in range(4):
        side(plane, z, QUAD * quad, QUAD, quad, 0, True).start()

    for load in loads:
        load.wait()
    stage_indices(own, type_count, ids, types, count, child, octant, stage)
    to_index = pltpu.make_async_copy(stage, index, stage_sem)
    to_index.start()
    build_interp(me_dir, stencil, weights, matrix)
    build_phases(angles, phase)
    broadcast_table(raw, table, type_count)
    to_index.wait()

    def ring_step(step, carry):
        for way in range(2):
            origin = (z + step) % RING if way else (z + RING - step) % RING
            code = reach_code(way, origin)
            from_x, from_y = place_of(origin)
            for quad in range(4):
                far = code // 16**quad % 16
                half_x, half_y = quad % 2, quad // 2
                same_x, same_y = from_x == dx, from_y == dy
                next_x = from_x - dx == 1 - 2 * half_x
                next_y = from_y - dy == 1 - 2 * half_y
                start = QUAD * quad

                @pl.when(step <= far)
                def _():
                    hop(way, step - 1, quad, origin).wait_recv()

                    @pl.when(step < far)
                    def _():
                        hop(way, step, quad, origin).start()

                    @pl.when(same_x & same_y)
                    def _():
                        side(plane, origin, start, 16, quad, 0).start()

                    @pl.when(same_x & next_y)
                    def _():
                        side(plane, origin, start + 8 * half_y, 8, quad, 0).start()

                    @pl.when(next_x & same_y)
                    def _():
                        side(plane, origin, start + 4 * half_x, 4, quad, 0).start()
                        side(plane, origin, start + 8 + 4 * half_x, 4, quad, 1).start()

                    @pl.when(next_x & next_y)
                    def _():
                        at = start + 4 * half_x + 8 * half_y
                        side(plane, origin, at, 4, quad, 0).start()

        return carry

    lax.fori_loop(1, HOPS + 1, ring_step, 0)

    def every_side(act, which_plane):
        for half in range(2):
            base = (z // 8 + half) % 2 * 8
            for quad in range(4):
                act(side(which_plane, base + z % 8, QUAD * quad, QUAD, quad, 0))
            across = base + z_of(dx, 1 - dy)
            for half_x in range(2):
                quad = half_x + 2 * dy
                act(side(which_plane, across, QUAD * quad + 8 * dy, 8, quad, 0))
            for half_x in range(2):
                to_x = dx + 1 - 2 * half_x

                @pl.when((to_x >= 0) & (to_x <= 3))
                def _():
                    beside = base + z_of(to_x, dy)
                    for half_y in range(2):
                        quad = half_x + 2 * half_y
                        start = QUAD * quad + 4 * half_x
                        act(side(which_plane, beside, start, 4, quad, 0))
                        act(side(which_plane, beside, start + 8, 4, quad, 1))
                    quad = half_x + 2 * dy
                    start = QUAD * quad + 4 * half_x + 8 * dy
                    act(side(which_plane, base + z_of(to_x, 1 - dy), start, 4, quad, 0))

    every_side(lambda copy: copy.wait_recv(), 1 - plane)

    translate_boxes(slots, index, field, table, moved)
    shift_children(index, moved, phase, shifted)

    def pack(chunk, carry):
        pack_rows(shifted, matrix, outbox, chunk)
        return carry

    lax.fori_loop(0, 4, pack, 0)

    def swap(to, source):
        return pltpu.make_async_remote_copy(
            src_ref=outbox.at[to],
            dst_ref=inbox.at[source],
            send_sem=swap_send.at[to],
            recv_sem=swap_recv.at[source],
            device_id={"dir": to},
            device_id_type=MESH,
        )

    def send(step, carry):
        swap((me_dir + step) % 16, me_dir).start()
        return carry

    lax.fori_loop(1, 16, send, 0)
    inbox[me_dir] = outbox[me_dir]

    every_side(lambda copy: copy.wait_send(), plane)

    def ring_drain(step, carry):
        for way in range(2):
            origin = (z + step) % RING if way else (z + RING - step) % RING
            code = reach_code(way, origin)
            for quad in range(4):

                @pl.when(step < code // 16**quad % 16)
                def _():
                    hop(way, step, quad, origin).wait_send()

        return carry

    lax.fori_loop(0, HOPS, ring_drain, 0)

    def receive(step, carry):
        other = (me_dir + step) % 16
        swap(other, other).wait_recv()
        swap(other, me_dir).wait_send()
        return carry

    lax.fori_loop(1, 16, receive, 0)
    assemble(inbox, out_ref)


def per_device(
    coarse_field,
    trans_table,
    partner_ids,
    partner_types,
    partner_count,
    child_count,
    child_octant,
    dir_angles,
    stencil_ids,
    stencil_weights,
):
    type_count = trans_table.shape[0]
    slots = partner_ids.shape[1]
    f32, i32 = jnp.float32, jnp.int32
    vmem, dma = pltpu.VMEM, pltpu.SemaphoreType.DMA
    return pl.pallas_call(
        functools.partial(kernel, type_count),
        out_shape=jax.ShapeDtypeStruct((16, 2, 4, 512), f32),
        in_specs=[pl.BlockSpec(memory_space=pl.ANY)] * 10,
        out_specs=pl.BlockSpec(memory_space=pltpu.VMEM),
        scratch_shapes=[
            vmem((2048, 8, 128), f32),
            vmem((2 * type_count, 128), f32),
            vmem((512, 2, 8, 128), f32),
            vmem((slots, TILE), i32),
            vmem((slots, TILE), i32),
            vmem((1, TILE), i32),
            vmem((1, TILE), i32),
            vmem((2, 128), i32),
            vmem((2, 128), f32),
            vmem((4, 128), i32),
            vmem((4, 128), f32),
            vmem((72, 128), i32),
            pltpu.SMEM((72, 128), i32),
            vmem((8, 2, 8, 128), f32),
            vmem((TILE, 2, 8, 128), f32),
            vmem((64, 8, 512), f32),
            vmem((256, 512), f32),
            vmem((16, 5, 8, 128), f32),
            vmem((16, 5, 8, 128), f32),
            dma((10,)),
            dma,
            dma((2, HOPS + 1, 4)),
            dma((2, HOPS + 1, 4)),
            dma((RING, 4, 2)),
            dma((RING, 4, 2)),
            dma((16,)),
            dma((16,)),
        ],
        compiler_params=pltpu.CompilerParams(collective_id=0, has_side_effects=True),
    )(
        coarse_field.reshape(TILE, 8, 128),
        trans_table.reshape(2 * type_count, 128),
        partner_ids.T,
        partner_types.T,
        partner_count.reshape(1, TILE),
        child_count.reshape(1, TILE),
        child_octant.reshape(2, 128),
        dir_angles,
        stencil_ids.T,
        stencil_weights.T,
    )


def solution(mesh):
    placed = (
        P("box", None, None, "dir"),
        P(None, None, "dir"),
        P("box", None),
        P("box", None),
        P("box"),
        P("box"),
        P("box"),
        P(),
        P(),
        P(),
    )
    return jax.shard_map(
        per_device,
        mesh=mesh,
        in_specs=placed,
        out_specs=P(("box", "dir"), None, None, None),
        check_vma=False,
    )
```

time: 436 us -> 82.3 us (0.19); the launches traced: 431 us -> 82.2 us
  local copies, waits for them, and re-layouts: 172 us -> 1.67 us
  waiting for transfers between devices: 145 us -> 0 us
  Pallas kernels: 0 us -> 80.5 us
  other arithmetic: 54.2 us -> 0 us
  starting transfers between devices: 28.3 us -> 0 us
  matrix products: 16.2 us -> 0 us
  between operations: 13.6 us -> 0.01 us
    gather x62 -> x0, local copies, waits for them, and re-layouts: 131 us -> none  [the longest x60 129 us: translate(): jnp.take(flat_sources, part_ids, axis=0)]
    all_gather x1 -> x0, waiting for transfers between devices: 127 us -> none  [per_device(): sources = lax.all_gather(coarse_field, 'box', axis=0, tiled=True)]
    pallas_call x0 -> x1, Pallas kernels: none -> 80.5 us  [per_device(): pl.pallas_call(functools.partial(kernel, type_count), out_shape=jax.Shape...]
    all_to_all x1 -> x0, starting transfers between devices: 28.3 us -> none  [per_device(): lax.all_to_all(shifted, 'dir', split_axis=0, concat_axis=3, tiled=True)]
    select_n x61 -> x0, other arithmetic: 24.8 us -> none  [the longest x60 24.8 us: translate(): jnp.take(flat_sources, part_ids, axis=0)]
    eq x30 -> x0, local copies, waits for them, and re-layouts: 20.9 us -> none  [translate(): type_ids[:, None] == type_range[None, :]]
    and x30 -> x0, other arithmetic: 20.9 us -> none  [translate(): jnp.take(flat_sources, part_ids, axis=0)]
    all_to_all x1 -> x0, waiting for transfers between devices: 17.2 us -> none  [per_device(): lax.all_to_all(shifted, 'dir', split_axis=0, concat_axis=3, tiled=True)]
  transfers between devices with their start and end apart: 2 -> 0, of which waited for: 2 -> 0; matrix products, arithmetic and copies ran while one was open for 2% -> 0% of each run, Pallas kernels for 0% -> 0%
where the time goes in v1:
time: 82.3 us; the launch traced here: 82.2 us
  Pallas kernels  80.5 us (98%)
  local copies, waits for them, and re-layouts  1.67 us (2%)
    pallas_call x1, Pallas kernels, per_device(): pl.pallas_call(functools.partial(kernel, type_count), out_shape=jax.Shape...  80.5 us
    unnamed x1, local copies, waits for them, and re-layouts  1.67 us

profile of v1, /device:TPU:1, one launch (start us, length us, event | category | flops | bytes accessed | tf_op | source)
XLA Modules:
  0.0 82.2 jit_solution(9579142526609675535)
XLA Ops:
  0.0 80.5 %shard_map.100 = f32[16,2,4,512]{3,2,1,0:T(4,128)} custom-call(f32[64,8,128]{2,1,0:T(8,128)} %bitcast.10, f32[632,128]{1,0:T(8,128)} %bitcast.9, s32[30,64]{1,0:T(8,128)} %bitcast.13, s32[30,64]{1,0:T(8,128)} %bitcast.14, s32[1,64]{1,0:T(1,128)} %bitcast.16, s32[1,64]{1,0:T(1,128)} %bitcast.17, s32[2,128]{1,0:T(2,128)} %bitcast.15, f32[2,2048]{1,0:T(2,128)} %angles_hbm.1, ...), custom_call_target="tpu_custom_call" | custom-call | tf_op jit(solution)/shard_map/pallas_call | solution.py:477
  80.5 1.7 %copy.12 = f32[16,2,4,512]{3,2,1,0:T(4,128)} copy(f32[16,2,4,512]{3,2,1,0:T(4,128)} %shard_map.100) | data formatting | bytes 524288

commit v2 on v1

--- a/solution.py
+++ b/solution.py
@@ -70,7 +70,7 @@
 
 
 def pack_rows(shifted_ref, matrix_ref, send_ref, chunk):
-    rows = shifted_ref[pl.ds(16 * chunk, 16)].reshape(128, 512)
+    rows = shifted_ref[...].reshape(128, 512)
     product = lax.dot_general(
         rows,
         matrix_ref[...],
@@ -124,10 +124,9 @@
 def broadcast_table(raw_ref, table_ref, type_count):
     def step(tile, carry):
         rows = raw_ref[pl.ds(8 * tile, 8), :]
-        for which in range(4):
-            for part in range(2):
-                at = 2 * which + part
-                table_ref[4 * tile + which, part] = jnp.broadcast_to(rows[at : at + 1], (8, 128))
+        for at in range(8):
+            row = jnp.broadcast_to(rows[at : at + 1], (8, 128))
+            table_ref[4 * tile + at // 2, at % 2] = row
         return carry
 
     lax.fori_loop(0, type_count // 4, step, 0)
@@ -139,16 +138,17 @@
     slot = lax.broadcasted_iota(jnp.int32, (slots, TILE), 0)
     box = lax.broadcasted_iota(jnp.int32, (slots, TILE), 1)
     live = slot < count_ref[...]
-    stage_ref[0:slots, 0:TILE] = jnp.where(live, ids_ref[...], own + box)
-    stage_ref[32 : 32 + slots, 0:TILE] = jnp.where(live, types_ref[...], type_count)
+    source = jnp.where(live, ids_ref[...], own + box)
+    kind = jnp.where(live, types_ref[...], type_count)
+    stage_ref[0:slots, 0:TILE] = source * 65536 + kind
     upto = lax.broadcasted_iota(jnp.int32, (TILE, TILE), 0)
     which = lax.broadcasted_iota(jnp.int32, (TILE, TILE), 1)
     bounds = jnp.sum(jnp.where(which <= upto, child_ref[...], 0), axis=1, keepdims=True)
     for half in range(2):
         fine = lax.broadcasted_iota(jnp.int32, (TILE, 128), 1) + 128 * half
         parent = jnp.sum(jnp.where(bounds <= fine, 1, 0), axis=0, keepdims=True)
-        stage_ref[64 + half : 65 + half, :] = jnp.minimum(parent, TILE - 1)
-    stage_ref[66:68, :] = octant_ref[...]
+        parent = jnp.minimum(parent, TILE - 1)
+        stage_ref[32 + half : 33 + half, :] = parent * 16 + octant_ref[half : half + 1, :]
 
 
 def build_phases(angle_ref, phase_ref):
@@ -174,8 +174,9 @@
     def step(box, carry):
         sums = [None] * 4
         for slot in range(slots):
-            source = field_ref[index_ref[slot, box] & (field_ref.shape[0] - 1)]
-            kind = index_ref[32 + slot, box] & (table_ref.shape[0] - 1)
+            packed = index_ref[slot, box]
+            source = field_ref[(packed >> 16) & (field_ref.shape[0] - 1)]
+            kind = packed & (table_ref.shape[0] - 1)
             for part in range(2):
                 term = table_ref[kind, part] * source
                 at = 2 * (slot % 2) + part
@@ -188,24 +189,21 @@
         moved_ref[box, 1] = pltpu.roll(value, 4, 0)
         return carry
 
-    lax.fori_loop(0, TILE, step, 0)
-
-
-def shift_children(index_ref, moved_ref, phase_ref, shifted_ref):
-    def step(owner, carry):
+    lax.fori_loop(0, TILE, step, 0, unroll=2)
+
+
+def shift_children(chunk, index_ref, moved_ref, phase_ref, shifted_ref):
+    for owner in range(4):
         for fine in range(16):
             sub, line = fine // 4, fine % 4
             at = 16 * owner + fine
-            parent = index_ref[64 + at // 128, at % 128] & (TILE - 1)
-            octant = index_ref[66 + at // 128, at % 128] & 7
+            packed = index_ref[32 + chunk // 2, 64 * (chunk % 2) + at]
+            parent, octant = (packed >> 4) & (TILE - 1), packed & 7
             value = (
                 moved_ref[parent, 0] * phase_ref[octant, 0]
                 + moved_ref[parent, 1] * phase_ref[octant, 1]
             )
             shifted_ref[4 * owner + line, :, 128 * sub : 128 * sub + 128] = value
-        return carry
-
-    lax.fori_loop(0, 16, step, 0)
 
 
 def kernel(
@@ -407,14 +405,6 @@
     every_side(lambda copy: copy.wait_recv(), 1 - plane)
 
     translate_boxes(slots, index, field, table, moved)
-    shift_children(index, moved, phase, shifted)
-
-    def pack(chunk, carry):
-        pack_rows(shifted, matrix, outbox, chunk)
-        return carry
-
-    lax.fori_loop(0, 4, pack, 0)
-
     def swap(to, source):
         return pltpu.make_async_remote_copy(
             src_ref=outbox.at[to],
@@ -425,11 +415,20 @@
             device_id_type=MESH,
         )
 
-    def send(step, carry):
-        swap((me_dir + step) % 16, me_dir).start()
+    def pack(step, carry):
+        chunk = (me_dir // 4 + 1 + step) % 4
+        shift_children(chunk, index, moved, phase, shifted)
+        pack_rows(shifted, matrix, outbox, chunk)
+        for owner in range(4):
+            to = 4 * chunk + owner
+
+            @pl.when(to != me_dir)
+            def _():
+                swap(to, me_dir).start()
+
         return carry
 
-    lax.fori_loop(1, 16, send, 0)
+    lax.fori_loop(0, 4, pack, 0)
     inbox[me_dir] = outbox[me_dir]
 
     every_side(lambda copy: copy.wait_send(), plane)
@@ -491,11 +490,11 @@
             vmem((2, 128), f32),
             vmem((4, 128), i32),
             vmem((4, 128), f32),
-            vmem((72, 128), i32),
-            pltpu.SMEM((72, 128), i32),
+            vmem((40, 128), i32),
+            pltpu.SMEM((40, 128), i32),
             vmem((8, 2, 8, 128), f32),
             vmem((TILE, 2, 8, 128), f32),
-            vmem((64, 8, 512), f32),
+            vmem((16, 8, 512), f32),
             vmem((256, 512), f32),
             vmem((16, 5, 8, 128), f32),
             vmem((16, 5, 8, 128), f32),

time: 82.3 us -> 77.2 us (0.938)
  Pallas kernels: 80.5 us -> 75.4 us
    pallas_call x1, Pallas kernels: 80.5 us -> 75.4 us  [per_device(): pl.pallas_call(functools.partial(kernel, type_count), out_shape=jax.Shape...]
where the time goes in v2:
time: 77.2 us; the launch traced here: 77.1 us
  Pallas kernels  75.4 us (98%)
  local copies, waits for them, and re-layouts  1.67 us (2%)
    pallas_call x1, Pallas kernels, per_device(): pl.pallas_call(functools.partial(kernel, type_count), out_shape=jax.Shape...  75.4 us
    unnamed x1, local copies, waits for them, and re-layouts  1.67 us

profile of v2, /device:TPU:1, one launch (start us, length us, event | category | flops | bytes accessed | tf_op | source)
XLA Modules:
  0.0 77.1 jit_solution(16725032096408604510)
XLA Ops:
  0.0 75.4 %shard_map.100 = f32[16,2,4,512]{3,2,1,0:T(4,128)} custom-call(f32[64,8,128]{2,1,0:T(8,128)} %bitcast.10, f32[632,128]{1,0:T(8,128)} %bitcast.9, s32[30,64]{1,0:T(8,128)} %bitcast.13, s32[30,64]{1,0:T(8,128)} %bitcast.14, s32[1,64]{1,0:T(1,128)} %bitcast.16, s32[1,64]{1,0:T(1,128)} %bitcast.17, s32[2,128]{1,0:T(2,128)} %bitcast.15, f32[2,2048]{1,0:T(2,128)} %angles_hbm.1, ...), custom_call_target="tpu_custom_call" | custom-call | tf_op jit(solution)/shard_map/pallas_call | solution.py:476
  75.4 1.7 %copy.12 = f32[16,2,4,512]{3,2,1,0:T(4,128)} copy(f32[16,2,4,512]{3,2,1,0:T(4,128)} %shard_map.100) | data formatting | bytes 524288

commit v3 on v2

--- a/solution.py
+++ b/solution.py
@@ -13,27 +13,54 @@
 RING = 16
 HOPS = 8
 TILE = 64
-QUAD = 16
+PART = 8
+PARTS = 8
 
 REACH = (
-    ((8, 0), (1, 8), (2, 8), (3, 8)),
-    ((8, 1), (3, 8), (8, 7), (5, 8)),
-    ((8, 2), (8, 7), (0, 8), (1, 8)),
-    ((8, 3), (6, 8), (8, 1), (3, 8)),
-    ((8, 3), (1, 8), (8, 6), (3, 8)),
-    ((8, 1), (8, 0), (7, 8), (2, 8)),
-    ((8, 5), (7, 8), (8, 3), (1, 8)),
-    ((8, 3), (8, 2), (8, 1), (0, 8)),
+    ((8, 0), (8, 0), (1, 8), (1, 8), (8, 0), (2, 8), (1, 8), (3, 8)),
+    ((8, 1), (8, 1), (3, 8), (3, 8), (8, 1), (8, 7), (3, 8), (8, 6)),
+    ((8, 2), (8, 0), (8, 7), (1, 8), (8, 0), (0, 8), (1, 8), (1, 8)),
+    ((8, 3), (8, 1), (6, 8), (3, 8), (8, 1), (8, 1), (8, 5), (3, 8)),
+    ((8, 3), (8, 3), (1, 8), (1, 8), (8, 3), (8, 6), (1, 8), (3, 8)),
+    ((8, 1), (8, 1), (0, 8), (0, 8), (8, 1), (8, 7), (0, 8), (2, 8)),
+    ((6, 8), (8, 3), (8, 7), (1, 8), (8, 3), (8, 3), (1, 8), (1, 8)),
+    ((8, 3), (8, 1), (8, 2), (0, 8), (8, 1), (8, 1), (0, 8), (0, 8)),
 )
 
-
-def reach_code(way, origin):
+ORDER = (
+    (5, 0),
+    (3, 1),
+    (4, 0),
+    (0, 1),
+    (0, 0),
+    (7, 1),
+    (7, 0),
+    (6, 0),
+    (1, 1),
+    (4, 1),
+    (2, 0),
+    (6, 1),
+    (3, 0),
+    (1, 0),
+    (5, 1),
+    (2, 1),
+)
+
+
+def reach_codes(way, origin):
     place = origin % 8
-    code = jnp.int32(0)
-    for which in range(8):
-        packed = sum(REACH[which][quad][way] * 16**quad for quad in range(4))
-        code = jnp.where(place == which, jnp.int32(packed), code)
-    return code
+    codes = []
+    for base in (0, 4):
+        code = jnp.int32(0)
+        for which in range(8):
+            packed = sum(REACH[which][base + at][way] * 16**at for at in range(4))
+            code = jnp.where(place == which, jnp.int32(packed), code)
+        codes.append(code)
+    return codes
+
+
+def reach_of(codes, part):
+    return codes[part // 4] // 16 ** (part % 4) % 16
 
 
 def place_of(z):
@@ -133,14 +160,17 @@
     table_ref[type_count] = jnp.zeros((2, 8, 128), jnp.float32)
 
 
-def stage_indices(own, type_count, ids_ref, types_ref, count_ref, child_ref, octant_ref, stage_ref):
+def stage_indices(
+    own, type_count, ids_ref, types_ref, count_ref, child_ref, octant_ref, work_ref, stage_ref
+):
     slots = ids_ref.shape[0]
     slot = lax.broadcasted_iota(jnp.int32, (slots, TILE), 0)
     box = lax.broadcasted_iota(jnp.int32, (slots, TILE), 1)
     live = slot < count_ref[...]
-    source = jnp.where(live, ids_ref[...], own + box)
-    kind = jnp.where(live, types_ref[...], type_count)
-    stage_ref[0:slots, 0:TILE] = source * 65536 + kind
+    work_ref[...] = jnp.zeros((128, 128), jnp.int32)
+    work_ref[0:slots, 0:TILE] = jnp.where(live, ids_ref[...], own + box)
+    work_ref[32 : 32 + slots, 0:TILE] = jnp.where(live, types_ref[...], type_count)
+    stage_ref[0:TILE, :] = work_ref[...].T[0:TILE]
     upto = lax.broadcasted_iota(jnp.int32, (TILE, TILE), 0)
     which = lax.broadcasted_iota(jnp.int32, (TILE, TILE), 1)
     bounds = jnp.sum(jnp.where(which <= upto, child_ref[...], 0), axis=1, keepdims=True)
@@ -148,7 +178,10 @@
         fine = lax.broadcasted_iota(jnp.int32, (TILE, 128), 1) + 128 * half
         parent = jnp.sum(jnp.where(bounds <= fine, 1, 0), axis=0, keepdims=True)
         parent = jnp.minimum(parent, TILE - 1)
-        stage_ref[32 + half : 33 + half, :] = parent * 16 + octant_ref[half : half + 1, :]
+        words = jnp.broadcast_to(parent * 16 + octant_ref[half : half + 1, :], (8, 128))
+        at = TILE + 2 * half
+        stage_ref[at : at + 1, :] = words[0:1]
+        stage_ref[at + 1 : at + 2, :] = pltpu.roll(words, 64, 1)[0:1]
 
 
 def build_phases(angle_ref, phase_ref):
@@ -174,9 +207,8 @@
     def step(box, carry):
         sums = [None] * 4
         for slot in range(slots):
-            packed = index_ref[slot, box]
-            source = field_ref[(packed >> 16) & (field_ref.shape[0] - 1)]
-            kind = packed & (table_ref.shape[0] - 1)
+            source = field_ref[index_ref[box, slot]]
+            kind = index_ref[box, 32 + slot]
             for part in range(2):
                 term = table_ref[kind, part] * source
                 at = 2 * (slot % 2) + part
@@ -189,7 +221,7 @@
         moved_ref[box, 1] = pltpu.roll(value, 4, 0)
         return carry
 
-    lax.fori_loop(0, TILE, step, 0, unroll=2)
+    lax.fori_loop(0, TILE, step, 0)
 
 
 def shift_children(chunk, index_ref, moved_ref, phase_ref, shifted_ref):
@@ -197,7 +229,7 @@
         for fine in range(16):
             sub, line = fine // 4, fine % 4
             at = 16 * owner + fine
-            packed = index_ref[32 + chunk // 2, 64 * (chunk % 2) + at]
+            packed = index_ref[TILE + chunk, at]
             parent, octant = (packed >> 4) & (TILE - 1), packed & 7
             value = (
                 moved_ref[parent, 0] * phase_ref[octant, 0]
@@ -230,6 +262,7 @@
     angles,
     stencil,
     weights,
+    work,
     stage,
     index,
     phase,
@@ -292,42 +325,42 @@
     def rows_of(which_plane, origin, start, size):
         return field.at[pl.ds(TILE * (RING * which_plane + origin) + start, size)]
 
-    def hop(way, step, quad, origin, first=False):
-        rows = rows_of(plane, origin, QUAD * quad, QUAD)
+    def hop(way, step, part, origin, first=False):
+        rows = rows_of(plane, origin, PART * part, PART)
         return pltpu.make_async_remote_copy(
-            src_ref=x_hbm.at[pl.ds(QUAD * quad, QUAD)] if first else rows,
+            src_ref=x_hbm.at[pl.ds(PART * part, PART)] if first else rows,
             dst_ref=rows,
-            send_sem=ring_send.at[way, step, quad],
-            recv_sem=ring_recv.at[way, step, quad],
+            send_sem=ring_send.at[way, step, part],
+            recv_sem=ring_recv.at[way, step, part],
             device_id={"box": RING * plane + (down if way else up)},
             device_id_type=MESH,
         )
 
-    def side(which_plane, origin, start, size, quad, part, first=False):
+    def side(which_plane, origin, part, shift, size, first=False):
+        start = PART * part + shift
         rows = rows_of(which_plane, origin, start, size)
         return pltpu.make_async_remote_copy(
             src_ref=x_hbm.at[pl.ds(start, size)] if first else rows,
             dst_ref=rows,
-            send_sem=side_send.at[origin, quad, part],
-            recv_sem=side_recv.at[origin, quad, part],
+            send_sem=side_send.at[origin, part],
+            recv_sem=side_recv.at[origin, part],
             device_id={"box": RING * (1 - plane) + z},
             device_id_type=MESH,
         )
 
-    for quad in (0, 3, 1, 2):
-        for way in range(2):
-            far = reach_code(way, z) // 16**quad % 16
-
-            @pl.when(far > 0)
-            def _():
-                hop(way, 0, quad, z, True).start()
-
-    for quad in range(4):
-        side(plane, z, QUAD * quad, QUAD, quad, 0, True).start()
+    first_codes = [reach_codes(way, z) for way in range(2)]
+    for part, way in ORDER:
+
+        @pl.when(reach_of(first_codes[way], part) > 0)
+        def _():
+            hop(way, 0, part, z, True).start()
+
+    for part in range(PARTS):
+        side(plane, z, part, 0, PART, True).start()
 
     for load in loads:
         load.wait()
-    stage_indices(own, type_count, ids, types, count, child, octant, stage)
+    stage_indices(own, type_count, ids, types, count, child, octant, work, stage)
     to_index = pltpu.make_async_copy(stage, index, stage_sem)
     to_index.start()
     build_interp(me_dir, stencil, weights, matrix)
@@ -336,43 +369,34 @@
     to_index.wait()
 
     def ring_step(step, carry):
-        for way in range(2):
-            origin = (z + step) % RING if way else (z + RING - step) % RING
-            code = reach_code(way, origin)
-            from_x, from_y = place_of(origin)
-            for quad in range(4):
-                far = code // 16**quad % 16
-                half_x, half_y = quad % 2, quad // 2
-                same_x, same_y = from_x == dx, from_y == dy
-                next_x = from_x - dx == 1 - 2 * half_x
-                next_y = from_y - dy == 1 - 2 * half_y
-                start = QUAD * quad
-
-                @pl.when(step <= far)
+        origins = [(z + RING - step) % RING, (z + step) % RING]
+        codes = [reach_codes(way, origins[way]) for way in range(2)]
+        spots = [place_of(origin) for origin in origins]
+        for part, way in ORDER:
+            origin, (from_x, from_y) = origins[way], spots[way]
+            far = reach_of(codes[way], part)
+            half_x, line = part // 2 % 2, part // 4 * 2 + part % 2
+            near_y = from_y == dy
+            if line == 0:
+                near_y = near_y | (from_y > dy)
+            if line == 3:
+                near_y = near_y | (from_y < dy)
+
+            @pl.when(step <= far)
+            def _():
+                hop(way, step - 1, part, origin).wait_recv()
+
+                @pl.when(step < far)
                 def _():
-                    hop(way, step - 1, quad, origin).wait_recv()
-
-                    @pl.when(step < far)
-                    def _():
-                        hop(way, step, quad, origin).start()
-
-                    @pl.when(same_x & same_y)
-                    def _():
-                        side(plane, origin, start, 16, quad, 0).start()
-
-                    @pl.when(same_x & next_y)
-                    def _():
-                        side(plane, origin, start + 8 * half_y, 8, quad, 0).start()
-
-                    @pl.when(next_x & same_y)
-                    def _():
-                        side(plane, origin, start + 4 * half_x, 4, quad, 0).start()
-                        side(plane, origin, start + 8 + 4 * half_x, 4, quad, 1).start()
-
-                    @pl.when(next_x & next_y)
-                    def _():
-                        at = start + 4 * half_x + 8 * half_y
-                        side(plane, origin, at, 4, quad, 0).start()
+                    hop(way, step, part, origin).start()
+
+                @pl.when(near_y & (from_x == dx))
+                def _():
+                    side(plane, origin, part, 0, PART).start()
+
+                @pl.when(near_y & (from_x - dx == 1 - 2 * half_x))
+                def _():
+                    side(plane, origin, part, 4 * half_x, 4).start()
 
         return carry
 
@@ -381,26 +405,21 @@
     def every_side(act, which_plane):
         for half in range(2):
             base = (z // 8 + half) % 2 * 8
-            for quad in range(4):
-                act(side(which_plane, base + z % 8, QUAD * quad, QUAD, quad, 0))
             across = base + z_of(dx, 1 - dy)
+            for part in range(PARTS):
+                act(side(which_plane, base + z % 8, part, 0, PART))
             for half_x in range(2):
-                quad = half_x + 2 * dy
-                act(side(which_plane, across, QUAD * quad + 8 * dy, 8, quad, 0))
+                act(side(which_plane, across, 5 * dy + 2 * half_x, 0, PART))
             for half_x in range(2):
                 to_x = dx + 1 - 2 * half_x
 
                 @pl.when((to_x >= 0) & (to_x <= 3))
                 def _():
-                    beside = base + z_of(to_x, dy)
-                    for half_y in range(2):
-                        quad = half_x + 2 * half_y
-                        start = QUAD * quad + 4 * half_x
-                        act(side(which_plane, beside, start, 4, quad, 0))
-                        act(side(which_plane, beside, start + 8, 4, quad, 1))
-                    quad = half_x + 2 * dy
-                    start = QUAD * quad + 4 * half_x + 8 * dy
-                    act(side(which_plane, base + z_of(to_x, 1 - dy), start, 4, quad, 0))
+                    for line in range(4):
+                        part = line // 2 * 4 + line % 2 + 2 * half_x
+                        act(side(which_plane, base + z_of(to_x, dy), part, 4 * half_x, 4))
+                    part = 5 * dy + 2 * half_x
+                    act(side(which_plane, base + z_of(to_x, 1 - dy), part, 4 * half_x, 4))
 
     every_side(lambda copy: copy.wait_recv(), 1 - plane)
 
@@ -436,12 +455,12 @@
     def ring_drain(step, carry):
         for way in range(2):
             origin = (z + step) % RING if way else (z + RING - step) % RING
-            code = reach_code(way, origin)
-            for quad in range(4):
-
-                @pl.when(step < code // 16**quad % 16)
+            codes = reach_codes(way, origin)
+            for part in range(PARTS):
+
+                @pl.when(step < reach_of(codes, part))
                 def _():
-                    hop(way, step, quad, origin).wait_send()
+                    hop(way, step, part, origin).wait_send()
 
         return carry
 
@@ -490,8 +509,9 @@
             vmem((2, 128), f32),
             vmem((4, 128), i32),
             vmem((4, 128), f32),
-            vmem((40, 128), i32),
-            pltpu.SMEM((40, 128), i32),
+            vmem((128, 128), i32),
+            vmem((72, 128), i32),
+            pltpu.SMEM((72, 128), i32),
             vmem((8, 2, 8, 128), f32),
             vmem((TILE, 2, 8, 128), f32),
             vmem((16, 8, 512), f32),
@@ -500,10 +520,10 @@
             vmem((16, 5, 8, 128), f32),
             dma((10,)),
             dma,
-            dma((2, HOPS + 1, 4)),
-            dma((2, HOPS + 1, 4)),
-            dma((RING, 4, 2)),
-            dma((RING, 4, 2)),
+            dma((2, HOPS + 1, PARTS)),
+            dma((2, HOPS + 1, PARTS)),
+            dma((RING, PARTS)),
+            dma((RING, PARTS)),
             dma((16,)),
             dma((16,)),
         ],

time: 77.2 us -> 73 us (0.946)
  Pallas kernels: 75.4 us -> 71.2 us
    pallas_call x1, Pallas kernels: 75.4 us -> 71.2 us  [per_device(): pl.pallas_call(functools.partial(kernel, type_count), out_shape=jax.Shape...]
where the time goes in v3:
time: 73 us; the launch traced here: 72.9 us
  Pallas kernels  71.2 us (98%)
  local copies, waits for them, and re-layouts  1.67 us (2%)
    pallas_call x1, Pallas kernels, per_device(): pl.pallas_call(functools.partial(kernel, type_count), out_shape=jax.Shape...  71.2 us
    unnamed x1, local copies, waits for them, and re-layouts  1.67 us

profile of v3, /device:TPU:1, one launch (start us, length us, event | category | flops | bytes accessed | tf_op | source)
XLA Modules:
  0.0 72.9 jit_solution(17238976405947081509)
XLA Ops:
  0.0 71.2 %shard_map.100 = f32[16,2,4,512]{3,2,1,0:T(4,128)} custom-call(f32[64,8,128]{2,1,0:T(8,128)} %bitcast.10, f32[632,128]{1,0:T(8,128)} %bitcast.9, s32[30,64]{1,0:T(8,128)} %bitcast.13, s32[30,64]{1,0:T(8,128)} %bitcast.14, s32[1,64]{1,0:T(1,128)} %bitcast.16, s32[1,64]{1,0:T(1,128)} %bitcast.17, s32[2,128]{1,0:T(2,128)} %bitcast.15, f32[2,2048]{1,0:T(2,128)} %angles_hbm.1, ...), custom_call_target="tpu_custom_call" | custom-call | tf_op jit(solution)/shard_map/pallas_call | solution.py:495
  71.2 1.7 %copy.12 = f32[16,2,4,512]{3,2,1,0:T(4,128)} copy(f32[16,2,4,512]{3,2,1,0:T(4,128)} %shard_map.100) | data formatting | bytes 524288

commit v4 on v3

--- a/solution.py
+++ b/solution.py
@@ -80,7 +80,12 @@
     return pltpu.roll(value, shift, 1) if shift else value
 
 
-def build_interp(me_dir, ids_ref, weights_ref, matrix_ref):
+def halves(value):
+    high = value.astype(jnp.bfloat16)
+    return high, (value - high.astype(jnp.float32)).astype(jnp.bfloat16)
+
+
+def build_interp(me_dir, ids_ref, weights_ref, high_ref, low_ref):
     relative = (ids_ref[...] - 32 * me_dir + 2 + 512) % 512
     weights = weights_ref[...]
     row = lax.broadcasted_iota(jnp.int32, (128, 128), 0)
@@ -92,19 +97,24 @@
             total = total + jnp.where(hit, weights[point : point + 1, :], 0.0)
         inner = (wanted >= 2) & (wanted < 34)
         columns = slice(128 * sub, 128 * sub + 128)
-        matrix_ref[0:128, columns] = jnp.where(inner, total, 0.0)
-        matrix_ref[128:256, columns] = jnp.where(inner, 0.0, total)
-
-
-def pack_rows(shifted_ref, matrix_ref, send_ref, chunk):
-    rows = shifted_ref[...].reshape(128, 512)
-    product = lax.dot_general(
-        rows,
-        matrix_ref[...],
-        (((1,), (1,)), ((), ())),
-        precision=lax.Precision.HIGHEST,
-        preferred_element_type=jnp.float32,
-    )
+        for at, value in (
+            (0, jnp.where(inner, total, 0.0)),
+            (128, jnp.where(inner, 0.0, total)),
+        ):
+            high, low = halves(value)
+            high_ref[at : at + 128, columns] = high
+            low_ref[at : at + 128, columns] = low
+
+
+def pack_rows(shifted_ref, high_ref, low_ref, send_ref, chunk):
+    high, low = halves(shifted_ref[...].reshape(128, 512))
+
+    def times(left, right):
+        return lax.dot_general(
+            left, right, (((1,), (1,)), ((), ())), preferred_element_type=jnp.float32
+        )
+
+    product = times(high, high_ref[...]) + times(high, low_ref[...]) + times(low, high_ref[...])
     for owner in range(4):
         edges = None
         for line in range(4):
@@ -168,8 +178,8 @@
     box = lax.broadcasted_iota(jnp.int32, (slots, TILE), 1)
     live = slot < count_ref[...]
     work_ref[...] = jnp.zeros((128, 128), jnp.int32)
-    work_ref[0:slots, 0:TILE] = jnp.where(live, ids_ref[...], own + box)
-    work_ref[32 : 32 + slots, 0:TILE] = jnp.where(live, types_ref[...], type_count)
+    source = jnp.where(live, ids_ref[...], own + box)
+    work_ref[0:slots, 0:TILE] = source * 65536 + jnp.where(live, types_ref[...], type_count)
     stage_ref[0:TILE, :] = work_ref[...].T[0:TILE]
     upto = lax.broadcasted_iota(jnp.int32, (TILE, TILE), 0)
     which = lax.broadcasted_iota(jnp.int32, (TILE, TILE), 1)
@@ -207,8 +217,9 @@
     def step(box, carry):
         sums = [None] * 4
         for slot in range(slots):
-            source = field_ref[index_ref[box, slot]]
-            kind = index_ref[box, 32 + slot]
+            packed = index_ref[box, slot]
+            source = field_ref[packed >> 16]
+            kind = packed & (table_ref.shape[0] - 1)
             for part in range(2):
                 term = table_ref[kind, part] * source
                 at = 2 * (slot % 2) + part
@@ -221,7 +232,7 @@
         moved_ref[box, 1] = pltpu.roll(value, 4, 0)
         return carry
 
-    lax.fori_loop(0, TILE, step, 0)
+    lax.fori_loop(0, TILE, step, 0, unroll=2)
 
 
 def shift_children(chunk, index_ref, moved_ref, phase_ref, shifted_ref):
@@ -268,7 +279,8 @@
     phase,
     moved,
     shifted,
-    matrix,
+    matrix_high,
+    matrix_low,
     outbox,
     inbox,
     load_sem,
@@ -330,20 +342,20 @@
         return pltpu.make_async_remote_copy(
             src_ref=x_hbm.at[pl.ds(PART * part, PART)] if first else rows,
             dst_ref=rows,
-            send_sem=ring_send.at[way, step, part],
+            send_sem=ring_send.at[way, part],
             recv_sem=ring_recv.at[way, step, part],
             device_id={"box": RING * plane + (down if way else up)},
             device_id_type=MESH,
         )
 
-    def side(which_plane, origin, part, shift, size, first=False):
+    def side(which_plane, origin, part, shift, size, slot, first=False):
         start = PART * part + shift
         rows = rows_of(which_plane, origin, start, size)
         return pltpu.make_async_remote_copy(
             src_ref=x_hbm.at[pl.ds(start, size)] if first else rows,
             dst_ref=rows,
-            send_sem=side_send.at[origin, part],
-            recv_sem=side_recv.at[origin, part],
+            send_sem=side_send.at[slot],
+            recv_sem=side_recv.at[slot],
             device_id={"box": RING * (1 - plane) + z},
             device_id_type=MESH,
         )
@@ -356,14 +368,14 @@
             hop(way, 0, part, z, True).start()
 
     for part in range(PARTS):
-        side(plane, z, part, 0, PART, True).start()
+        side(plane, z, part, 0, PART, part, True).start()
 
     for load in loads:
         load.wait()
     stage_indices(own, type_count, ids, types, count, child, octant, work, stage)
     to_index = pltpu.make_async_copy(stage, index, stage_sem)
     to_index.start()
-    build_interp(me_dir, stencil, weights, matrix)
+    build_interp(me_dir, stencil, weights, matrix_high, matrix_low)
     build_phases(angles, phase)
     broadcast_table(raw, table, type_count)
     to_index.wait()
@@ -376,7 +388,8 @@
             origin, (from_x, from_y) = origins[way], spots[way]
             far = reach_of(codes[way], part)
             half_x, line = part // 2 % 2, part // 4 * 2 + part % 2
-            near_y = from_y == dy
+            near_y = same_y = from_y == dy
+            base = jnp.where(origin // 8 == z // 8, 0, 20)
             if line == 0:
                 near_y = near_y | (from_y > dy)
             if line == 3:
@@ -392,11 +405,13 @@
 
                 @pl.when(near_y & (from_x == dx))
                 def _():
-                    side(plane, origin, part, 0, PART).start()
+                    slot = base + jnp.where(same_y, part, 8 + half_x)
+                    side(plane, origin, part, 0, PART, slot).start()
 
                 @pl.when(near_y & (from_x - dx == 1 - 2 * half_x))
                 def _():
-                    side(plane, origin, part, 4 * half_x, 4).start()
+                    slot = base + jnp.where(same_y, 10 + 4 * half_x + line, 18 + half_x)
+                    side(plane, origin, part, 4 * half_x, 4, slot).start()
 
         return carry
 
@@ -407,19 +422,22 @@
             base = (z // 8 + half) % 2 * 8
             across = base + z_of(dx, 1 - dy)
             for part in range(PARTS):
-                act(side(which_plane, base + z % 8, part, 0, PART))
+                act(side(which_plane, base + z % 8, part, 0, PART, 20 * half + part))
             for half_x in range(2):
-                act(side(which_plane, across, 5 * dy + 2 * half_x, 0, PART))
+                slot = 20 * half + 8 + half_x
+                act(side(which_plane, across, 5 * dy + 2 * half_x, 0, PART, slot))
             for half_x in range(2):
                 to_x = dx + 1 - 2 * half_x
 
                 @pl.when((to_x >= 0) & (to_x <= 3))
                 def _():
+                    shift = 4 * half_x
                     for line in range(4):
                         part = line // 2 * 4 + line % 2 + 2 * half_x
-                        act(side(which_plane, base + z_of(to_x, dy), part, 4 * half_x, 4))
-                    part = 5 * dy + 2 * half_x
-                    act(side(which_plane, base + z_of(to_x, 1 - dy), part, 4 * half_x, 4))
+                        slot = 20 * half + 10 + 4 * half_x + line
+                        act(side(which_plane, base + z_of(to_x, dy), part, shift, 4, slot))
+                    part, slot = 5 * dy + 2 * half_x, 20 * half + 18 + half_x
+                    act(side(which_plane, base + z_of(to_x, 1 - dy), part, shift, 4, slot))
 
     every_side(lambda copy: copy.wait_recv(), 1 - plane)
 
@@ -437,7 +455,7 @@
     def pack(step, carry):
         chunk = (me_dir // 4 + 1 + step) % 4
         shift_children(chunk, index, moved, phase, shifted)
-        pack_rows(shifted, matrix, outbox, chunk)
+        pack_rows(shifted, matrix_high, matrix_low, outbox, chunk)
         for owner in range(4):
             to = 4 * chunk + owner
 
@@ -452,19 +470,29 @@
 
     every_side(lambda copy: copy.wait_send(), plane)
 
-    def ring_drain(step, carry):
-        for way in range(2):
+    for way in range(2):
+        def count(step, sent):
             origin = (z + step) % RING if way else (z + RING - step) % RING
             codes = reach_codes(way, origin)
-            for part in range(PARTS):
-
-                @pl.when(step < reach_of(codes, part))
+            return tuple(
+                sent[part] + jnp.where(step < reach_of(codes, part), 1, 0) for part in range(PARTS)
+            )
+
+        sent = lax.fori_loop(0, HOPS, count, (jnp.int32(0),) * PARTS)
+        for part in range(PARTS):
+            for total in range(1, HOPS + 1):
+
+                @pl.when(sent[part] == total)
                 def _():
-                    hop(way, step, part, origin).wait_send()
-
-        return carry
-
-    lax.fori_loop(0, HOPS, ring_drain, 0)
+                    rows = field.at[pl.ds(0, PART * total)]
+                    pltpu.make_async_remote_copy(
+                        src_ref=rows,
+                        dst_ref=rows,
+                        send_sem=ring_send.at[way, part],
+                        recv_sem=ring_recv.at[way, 0, part],
+                        device_id={"box": RING * plane + (down if way else up)},
+                        device_id_type=MESH,
+                    ).wait_send()
 
     def receive(step, carry):
         other = (me_dir + step) % 16
@@ -515,15 +543,16 @@
             vmem((8, 2, 8, 128), f32),
             vmem((TILE, 2, 8, 128), f32),
             vmem((16, 8, 512), f32),
-            vmem((256, 512), f32),
+            vmem((256, 512), jnp.bfloat16),
+            vmem((256, 512), jnp.bfloat16),
             vmem((16, 5, 8, 128), f32),
             vmem((16, 5, 8, 128), f32),
             dma((10,)),
             dma,
-            dma((2, HOPS + 1, PARTS)),
-            dma((2, HOPS + 1, PARTS)),
-            dma((RING, PARTS)),
-            dma((RING, PARTS)),
+            dma((2, PARTS)),
+            dma((2, HOPS, PARTS)),
+            dma((40,)),
+            dma((40,)),
             dma((16,)),
             dma((16,)),
         ],

time: 73 us -> 69.3 us (0.949)
  Pallas kernels: 71.2 us -> 67.4 us
    pallas_call x1, Pallas kernels: 71.2 us -> 67.4 us  [per_device(): pl.pallas_call(functools.partial(kernel, type_count), out_shape=jax.Shape...]
where the time goes in v4:
time: 69.3 us; the launch traced here: 69.1 us
  Pallas kernels  67.4 us (97%)
  local copies, waits for them, and re-layouts  1.67 us (2%)
    pallas_call x1, Pallas kernels, per_device(): pl.pallas_call(functools.partial(kernel, type_count), out_shape=jax.Shape...  67.4 us
    unnamed x1, local copies, waits for them, and re-layouts  1.67 us

profile of v4, /device:TPU:1, one launch (start us, length us, event | category | flops | bytes accessed | tf_op | source)
XLA Modules:
  0.0 69.1 jit_solution(3423413279254377006)
XLA Ops:
  0.0 67.4 %shard_map.100 = f32[16,2,4,512]{3,2,1,0:T(4,128)} custom-call(f32[64,8,128]{2,1,0:T(8,128)} %bitcast.10, f32[632,128]{1,0:T(8,128)} %bitcast.9, s32[30,64]{1,0:T(8,128)} %bitcast.13, s32[30,64]{1,0:T(8,128)} %bitcast.14, s32[1,64]{1,0:T(1,128)} %bitcast.16, s32[1,64]{1,0:T(1,128)} %bitcast.17, s32[2,128]{1,0:T(2,128)} %bitcast.15, f32[2,2048]{1,0:T(2,128)} %angles_hbm.1, ...), custom_call_target="tpu_custom_call" | custom-call | tf_op jit(solution)/shard_map/pallas_call | solution.py:523
  67.4 1.7 %copy.12 = f32[16,2,4,512]{3,2,1,0:T(4,128)} copy(f32[16,2,4,512]{3,2,1,0:T(4,128)} %shard_map.100) | data formatting | bytes 524288

commit v5 on v4

--- a/solution.py
+++ b/solution.py
@@ -158,16 +158,9 @@
                 out_ref[4 * sub + line, 1, :, columns] = value[4:8]
 
 
-def broadcast_table(raw_ref, table_ref, type_count):
-    def step(tile, carry):
-        rows = raw_ref[pl.ds(8 * tile, 8), :]
-        for at in range(8):
-            row = jnp.broadcast_to(rows[at : at + 1], (8, 128))
-            table_ref[4 * tile + at // 2, at % 2] = row
-        return carry
-
-    lax.fori_loop(0, type_count // 4, step, 0)
-    table_ref[type_count] = jnp.zeros((2, 8, 128), jnp.float32)
+def fetch_operators(slots, box, index_ref, raw_ref, rows_ref):
+    for slot in range(slots):
+        rows_ref[box, 2 * slot : 2 * slot + 2, :] = raw_ref[index_ref[box, 32 + slot]]
 
 
 def stage_indices(
@@ -179,7 +172,8 @@
     live = slot < count_ref[...]
     work_ref[...] = jnp.zeros((128, 128), jnp.int32)
     source = jnp.where(live, ids_ref[...], own + box)
-    work_ref[0:slots, 0:TILE] = source * 65536 + jnp.where(live, types_ref[...], type_count)
+    work_ref[0:slots, 0:TILE] = source
+    work_ref[32 : 32 + slots, 0:TILE] = jnp.where(live, types_ref[...], type_count)
     stage_ref[0:TILE, :] = work_ref[...].T[0:TILE]
     upto = lax.broadcasted_iota(jnp.int32, (TILE, TILE), 0)
     which = lax.broadcasted_iota(jnp.int32, (TILE, TILE), 1)
@@ -211,17 +205,16 @@
         phase_ref[which, 1] = jnp.where(octant < 4, spread, -spread)
 
 
-def translate_boxes(slots, index_ref, field_ref, table_ref, moved_ref):
+def translate_boxes(slots, index_ref, field_ref, rows_ref, moved_ref):
     real_row = lax.broadcasted_iota(jnp.int32, (8, 128), 0) < 4
 
     def step(box, carry):
         sums = [None] * 4
         for slot in range(slots):
-            packed = index_ref[box, slot]
-            source = field_ref[packed >> 16]
-            kind = packed & (table_ref.shape[0] - 1)
+            source = field_ref[index_ref[box, slot]]
             for part in range(2):
-                term = table_ref[kind, part] * source
+                row = rows_ref[box, 2 * slot + part : 2 * slot + part + 1, :]
+                term = jnp.broadcast_to(row, (8, 128)) * source
                 at = 2 * (slot % 2) + part
                 sums[at] = term if sums[at] is None else sums[at] + term
         straight = sums[0] if sums[2] is None else sums[0] + sums[2]
@@ -264,7 +257,7 @@
     out_ref,
     field,
     raw,
-    table,
+    rows,
     ids,
     types,
     count,
@@ -305,7 +298,7 @@
         for at, (src, dst) in enumerate(
             (
                 (x_hbm, field.at[pl.ds(own, TILE)]),
-                (table_hbm, raw),
+                (table_hbm, raw.at[pl.ds(0, type_count)]),
                 (ids_hbm, ids),
                 (types_hbm, types),
                 (count_hbm, count),
@@ -338,10 +331,10 @@
         return field.at[pl.ds(TILE * (RING * which_plane + origin) + start, size)]
 
     def hop(way, step, part, origin, first=False):
-        rows = rows_of(plane, origin, PART * part, PART)
+        here = rows_of(plane, origin, PART * part, PART)
         return pltpu.make_async_remote_copy(
-            src_ref=x_hbm.at[pl.ds(PART * part, PART)] if first else rows,
-            dst_ref=rows,
+            src_ref=x_hbm.at[pl.ds(PART * part, PART)] if first else here,
+            dst_ref=here,
             send_sem=ring_send.at[way, part],
             recv_sem=ring_recv.at[way, step, part],
             device_id={"box": RING * plane + (down if way else up)},
@@ -377,14 +370,14 @@
     to_index.start()
     build_interp(me_dir, stencil, weights, matrix_high, matrix_low)
     build_phases(angles, phase)
-    broadcast_table(raw, table, type_count)
+    raw[type_count] = jnp.zeros((2, 128), jnp.float32)
     to_index.wait()
 
     def ring_step(step, carry):
         origins = [(z + RING - step) % RING, (z + step) % RING]
         codes = [reach_codes(way, origins[way]) for way in range(2)]
         spots = [place_of(origin) for origin in origins]
-        for part, way in ORDER:
+        for turn, (part, way) in enumerate(ORDER):
             origin, (from_x, from_y) = origins[way], spots[way]
             far = reach_of(codes[way], part)
             half_x, line = part // 2 % 2, part // 4 * 2 + part % 2
@@ -412,6 +405,9 @@
                 def _():
                     slot = base + jnp.where(same_y, 10 + 4 * half_x + line, 18 + half_x)
                     side(plane, origin, part, 4 * half_x, 4, slot).start()
+
+            if turn % 2:
+                fetch_operators(slots, 8 * (step - 1) + turn // 2, index, raw, rows)
 
         return carry
 
@@ -441,7 +437,7 @@
 
     every_side(lambda copy: copy.wait_recv(), 1 - plane)
 
-    translate_boxes(slots, index, field, table, moved)
+    translate_boxes(slots, index, field, rows, moved)
     def swap(to, source):
         return pltpu.make_async_remote_copy(
             src_ref=outbox.at[to],
@@ -527,8 +523,8 @@
         out_specs=pl.BlockSpec(memory_space=pltpu.VMEM),
         scratch_shapes=[
             vmem((2048, 8, 128), f32),
-            vmem((2 * type_count, 128), f32),
-            vmem((512, 2, 8, 128), f32),
+            vmem((type_count + 4, 2, 128), f32),
+            vmem((TILE, 64, 128), f32),
             vmem((slots, TILE), i32),
             vmem((slots, TILE), i32),
             vmem((1, TILE), i32),
@@ -559,7 +555,7 @@
         compiler_params=pltpu.CompilerParams(collective_id=0, has_side_effects=True),
     )(
         coarse_field.reshape(TILE, 8, 128),
-        trans_table.reshape(2 * type_count, 128),
+        trans_table,
         partner_ids.T,
         partner_types.T,
         partner_count.reshape(1, TILE),

time: 69.3 us -> 67.6 us (0.975)
  Pallas kernels: 67.4 us -> 65.8 us
    pallas_call x1, Pallas kernels: 67.4 us -> 65.8 us  [per_device(): pl.pallas_call(functools.partial(kernel, type_count), out_shape=jax.Shape...]
where the time goes in v5:
time: 67.6 us; the launch traced here: 67.5 us
  Pallas kernels  65.8 us (97%)
  local copies, waits for them, and re-layouts  1.67 us (2%)
    pallas_call x1, Pallas kernels, per_device(): pl.pallas_call(functools.partial(kernel, type_count), out_shape=jax.Shape...  65.8 us
    unnamed x1, local copies, waits for them, and re-layouts  1.67 us

profile of v5, /device:TPU:1, one launch (start us, length us, event | category | flops | bytes accessed | tf_op | source)
XLA Modules:
  0.0 67.5 jit_solution(16841190437722471214)
XLA Ops:
  0.0 65.8 %shard_map.100 = f32[16,2,4,512]{3,2,1,0:T(4,128)} custom-call(f32[64,8,128]{2,1,0:T(8,128)} %bitcast.8, f32[316,2,128]{2,1,0:T(2,128)} %table_hbm.1, s32[30,64]{1,0:T(8,128)} %bitcast.11, s32[30,64]{1,0:T(8,128)} %bitcast.12, s32[1,64]{1,0:T(1,128)} %bitcast.14, s32[1,64]{1,0:T(1,128)} %bitcast.15, s32[2,128]{1,0:T(2,128)} %bitcast.13, ...), custom_call_target="tpu_custom_call" | custom-call | tf_op jit(solution)/shard_map/pallas_call | solution.py:519
  65.8 1.7 %copy.12 = f32[16,2,4,512]{3,2,1,0:T(4,128)} copy(f32[16,2,4,512]{3,2,1,0:T(4,128)} %shard_map.100) | data formatting | bytes 524288

commit v6 on v5

--- a/solution.py
+++ b/solution.py
@@ -18,32 +18,32 @@
 
 REACH = (
     ((8, 0), (8, 0), (1, 8), (1, 8), (8, 0), (2, 8), (1, 8), (3, 8)),
-    ((8, 1), (8, 1), (3, 8), (3, 8), (8, 1), (8, 7), (3, 8), (8, 6)),
-    ((8, 2), (8, 0), (8, 7), (1, 8), (8, 0), (0, 8), (1, 8), (1, 8)),
-    ((8, 3), (8, 1), (6, 8), (3, 8), (8, 1), (8, 1), (8, 5), (3, 8)),
-    ((8, 3), (8, 3), (1, 8), (1, 8), (8, 3), (8, 6), (1, 8), (3, 8)),
-    ((8, 1), (8, 1), (0, 8), (0, 8), (8, 1), (8, 7), (0, 8), (2, 8)),
+    ((8, 1), (8, 1), (3, 8), (3, 8), (8, 1), (7, 8), (3, 8), (8, 6)),
+    ((8, 2), (8, 0), (7, 8), (1, 8), (8, 0), (8, 0), (1, 8), (1, 8)),
+    ((8, 3), (8, 1), (6, 8), (3, 8), (8, 1), (8, 1), (3, 8), (3, 8)),
+    ((8, 3), (8, 3), (1, 8), (1, 8), (5, 8), (8, 6), (1, 8), (3, 8)),
+    ((8, 1), (8, 1), (8, 0), (0, 8), (8, 1), (7, 8), (0, 8), (2, 8)),
     ((6, 8), (8, 3), (8, 7), (1, 8), (8, 3), (8, 3), (1, 8), (1, 8)),
     ((8, 3), (8, 1), (8, 2), (0, 8), (8, 1), (8, 1), (0, 8), (0, 8)),
 )
 
 ORDER = (
-    (5, 0),
+    (2, 1),
+    (4, 1),
+    (2, 0),
+    (7, 0),
+    (6, 1),
+    (1, 0),
+    (5, 1),
+    (3, 0),
+    (4, 0),
     (3, 1),
-    (4, 0),
+    (1, 1),
     (0, 1),
     (0, 0),
     (7, 1),
-    (7, 0),
+    (5, 0),
     (6, 0),
-    (1, 1),
-    (4, 1),
-    (2, 0),
-    (6, 1),
-    (3, 0),
-    (1, 0),
-    (5, 1),
-    (2, 1),
 )
 
 
@@ -373,6 +373,12 @@
     raw[type_count] = jnp.zeros((2, 128), jnp.float32)
     to_index.wait()
 
+    def fetch(box, carry):
+        fetch_operators(slots, box, index, raw, rows)
+        return carry
+
+    lax.fori_loop(0, TILE // 2, fetch, 0, unroll=2)
+
     def ring_step(step, carry):
         origins = [(z + RING - step) % RING, (z + step) % RING]
         codes = [reach_codes(way, origins[way]) for way in range(2)]
@@ -406,8 +412,10 @@
                     slot = base + jnp.where(same_y, 10 + 4 * half_x + line, 18 + half_x)
                     side(plane, origin, part, 4 * half_x, 4, slot).start()
 
-            if turn % 2:
-                fetch_operators(slots, 8 * (step - 1) + turn // 2, index, raw, rows)
+            @pl.when(step <= 2)
+            def _():
+                box = jnp.minimum(16 * (step + 1) + turn, TILE - 1)
+                fetch_operators(slots, box, index, raw, rows)
 
         return carry
 

time: 67.6 us -> 66.1 us (0.978)
  Pallas kernels: 65.8 us -> 64.2 us
    pallas_call x1, Pallas kernels: 65.8 us -> 64.2 us  [per_device(): pl.pallas_call(functools.partial(kernel, type_count), out_shape=jax.Shape...]
where the time goes in v6:
time: 66.1 us; the launch traced here: 65.9 us
  Pallas kernels  64.2 us (97%)
  local copies, waits for them, and re-layouts  1.67 us (3%)
    pallas_call x1, Pallas kernels, per_device(): pl.pallas_call(functools.partial(kernel, type_count), out_shape=jax.Shape...  64.2 us
    unnamed x1, local copies, waits for them, and re-layouts  1.67 us

profile of v6, /device:TPU:1, one launch (start us, length us, event | category | flops | bytes accessed | tf_op | source)
XLA Modules:
  0.0 65.9 jit_solution(18442235165379281483)
XLA Ops:
  0.0 64.2 %shard_map.100 = f32[16,2,4,512]{3,2,1,0:T(4,128)} custom-call(f32[64,8,128]{2,1,0:T(8,128)} %bitcast.8, f32[316,2,128]{2,1,0:T(2,128)} %table_hbm.1, s32[30,64]{1,0:T(8,128)} %bitcast.11, s32[30,64]{1,0:T(8,128)} %bitcast.12, s32[1,64]{1,0:T(1,128)} %bitcast.14, s32[1,64]{1,0:T(1,128)} %bitcast.15, s32[2,128]{1,0:T(2,128)} %bitcast.13, ...), custom_call_target="tpu_custom_call" | custom-call | tf_op jit(solution)/shard_map/pallas_call | solution.py:527
  64.3 1.7 %copy.12 = f32[16,2,4,512]{3,2,1,0:T(4,128)} copy(f32[16,2,4,512]{3,2,1,0:T(4,128)} %shard_map.100) | data formatting | bytes 524288

commit v7 on v6

--- a/solution.py
+++ b/solution.py
@@ -377,13 +377,13 @@
         fetch_operators(slots, box, index, raw, rows)
         return carry
 
-    lax.fori_loop(0, TILE // 2, fetch, 0, unroll=2)
+    lax.fori_loop(0, TILE, fetch, 0, unroll=2)
 
     def ring_step(step, carry):
         origins = [(z + RING - step) % RING, (z + step) % RING]
         codes = [reach_codes(way, origins[way]) for way in range(2)]
         spots = [place_of(origin) for origin in origins]
-        for turn, (part, way) in enumerate(ORDER):
+        for part, way in ORDER:
             origin, (from_x, from_y) = origins[way], spots[way]
             far = reach_of(codes[way], part)
             half_x, line = part // 2 % 2, part // 4 * 2 + part % 2
@@ -411,11 +411,6 @@
                 def _():
                     slot = base + jnp.where(same_y, 10 + 4 * half_x + line, 18 + half_x)
                     side(plane, origin, part, 4 * half_x, 4, slot).start()
-
-            @pl.when(step <= 2)
-            def _():
-                box = jnp.minimum(16 * (step + 1) + turn, TILE - 1)
-                fetch_operators(slots, box, index, raw, rows)
 
         return carry
 

time: 66.1 us -> 66.1 us (level)
  no operation moved by 1% of the time
where the time goes in v7:
time: 66.1 us; the launch traced here: 65.9 us
  Pallas kernels  64.2 us (97%)
  local copies, waits for them, and re-layouts  1.67 us (3%)
    pallas_call x1, Pallas kernels, per_device(): pl.pallas_call(functools.partial(kernel, type_count), out_shape=jax.Shape...  64.2 us
    unnamed x1, local copies, waits for them, and re-layouts  1.67 us

profile of v7, /device:TPU:1, one launch (start us, length us, event | category | flops | bytes accessed | tf_op | source)
XLA Modules:
  0.0 65.9 jit_solution(990261126734886198)
XLA Ops:
  0.0 64.2 %shard_map.100 = f32[16,2,4,512]{3,2,1,0:T(4,128)} custom-call(f32[64,8,128]{2,1,0:T(8,128)} %bitcast.8, f32[316,2,128]{2,1,0:T(2,128)} %table_hbm.1, s32[30,64]{1,0:T(8,128)} %bitcast.11, s32[30,64]{1,0:T(8,128)} %bitcast.12, s32[1,64]{1,0:T(1,128)} %bitcast.14, s32[1,64]{1,0:T(1,128)} %bitcast.15, s32[2,128]{1,0:T(2,128)} %bitcast.13, ...), custom_call_target="tpu_custom_call" | custom-call | tf_op jit(solution)/shard_map/pallas_call | solution.py:522
  64.2 1.7 %copy.12 = f32[16,2,4,512]{3,2,1,0:T(4,128)} copy(f32[16,2,4,512]{3,2,1,0:T(4,128)} %shard_map.100) | data formatting | bytes 524288
